TPU v7x, 32 devices: a whole 2x2x4 slice. The times are simulated.
32 devices in a mesh: row: 4 (over y, x), col: 8 (over z, core).
Axes of the slice: x: 2, y: 2, z: 4, core: 2. Of those that a mesh axis runs over, the one named last changes fastest.
Arguments:
- trail: float32 [2, 4, 512, 2, 8, 512], P(None, 'row', None, None, 'col'), may hold values from -6 to 6
- panel: float32 [2, 4, 512, 512], P(None, 'row', None, 'col'), may hold values from -6 to 6
- row_basis: float32 [2, 4, 64, 512], P(None, 'row', None, 'col'), may hold values from -0.75 to 0.75
- row_coeff: float32 [2, 4, 64, 512], P(None, 'row', None, 'col'), may hold values from -0.25 to 0.25
- col_basis: float32 [2, 8, 64, 512], P(None, 'col', None, 'row'), may hold values from -0.75 to 0.75
- col_scaled: float32 [2, 8, 64, 512], P(None, 'col', None, 'row'), may hold values from -0.25 to 0.25
- pivot_basis: float32 [64, 512], P(None, 'col'), may hold values from -0.75 to 0.75
- pivot_scaled: float32 [64, 512], replicated, may hold values from -0.25 to 0.25
- sketch: float32 [64, 512], replicated, may hold values from -6 to 6
- perm: int32 [512], replicated, may hold values from 0 to 511, each once
- pair_kind: int32 [256], replicated, may hold values from 0 to 1
- pivot_values: float32 [3, 256], replicated, may hold values from -3 to 3, as said below
Outputs:
- trail_out: float32 [2, 4, 512, 2, 8, 512], P(None, 'row', None, None, 'col')
- basis_out: float32 [2, 4, 64, 512], P(None, 'row')
- coeff_out: float32 [2, 4, 64, 512], P(None, 'row')
Inputs may be any that keep to these rules, and one draw needn't show every extreme that they name: `pivot_values`: rows 0 and 1 have magnitudes between 0.5 and 0.7; row 2 has magnitude 1.2 or more.
All inputs are finite; a program needn't handle non-finite values.
Results may differ from a plain program's by a relative error of at most 0.00013.
Values sent between devices are 32-bit elements; how exact they have to be, the bound alone decides.
No kernel may reach another device: no remote copies, remote signals or barrier semaphores. Data moves between devices by JAX's collectives and lax.ppermute only.
A program may use at most 64 MiB of HBM per device.

v0:
```python
import jax
import jax.numpy as jnp
from jax import lax
from jax.sharding import PartitionSpec as P


def pair_apply(rows, pair_kind, pivot_values):
    shaped = rows.reshape(rows.shape[:-1] + (rows.shape[-1] // 2, 2))
    first_in = shaped[..., 0]
    second_in = shaped[..., 1]
    diag_one = pivot_values[0]
    diag_two = pivot_values[1]
    offdiag = pivot_values[2]
    determinant = diag_one * diag_two - offdiag * offdiag
    twin = pair_kind == 1
    first = jnp.where(
        twin, (first_in * diag_two - second_in * offdiag) / determinant, first_in / diag_one
    )
    second = jnp.where(
        twin, (second_in * diag_one - first_in * offdiag) / determinant, second_in / diag_two
    )
    return jnp.stack([first, second], axis=-1).reshape(rows.shape)


def tri_solve(lower, rhs):
    return jax.vmap(lambda low, right: jax.scipy.linalg.solve_triangular(low, right, lower=True))(
        lower, rhs
    )


def body(
    trail,
    panel,
    row_basis,
    row_coeff,
    col_basis,
    col_scaled,
    pivot_basis,
    pivot_scaled,
    sketch,
    perm,
    pair_kind,
    pivot_values,
):
    highest = lax.Precision.HIGHEST
    width = sketch.shape[1]
    block = panel.shape[3]
    xrows, yrows = (
        lax.all_gather(row_basis, "col", axis=3, tiled=True),
        lax.all_gather(row_coeff, "col", axis=3, tiled=True),
    )
    zcols, gcols = (
        lax.all_gather(col_basis, "row", axis=3, tiled=True),
        lax.all_gather(col_scaled, "row", axis=3, tiled=True),
    )
    xrows = xrows[:, 0]
    yrows = yrows[:, 0]
    zcols = zcols[:, 0]
    gcols = gcols[:, 0]
    core = jnp.einsum("arp,bsp->arbs", yrows, gcols, precision=highest)
    left = jnp.einsum("arp,arbs->apbs", xrows, core, precision=highest)
    change = jnp.einsum("apbs,bsq->apbq", left, zcols, precision=highest)
    trail_out = trail - change[:, None, :, :, None, :]
    pcore = jnp.einsum("arp,sp->ars", yrows, pivot_scaled, precision=highest)
    pleft = jnp.einsum("arp,ars->aps", xrows, pcore, precision=highest)
    updated = panel[:, 0] - jnp.einsum("aps,sq->apq", pleft, pivot_basis, precision=highest)
    scaled_t = pair_apply(sketch, pair_kind, pivot_values)
    column_ids = lax.axis_index("col") * block + jnp.arange(block, dtype=jnp.int32)
    selector = (perm[:, None] == column_ids[None, :]).astype(jnp.float32)
    local_sketch = jnp.dot(scaled_t, selector, precision=highest)
    partial_range = jnp.einsum("apq,rq->arp", updated, local_sketch, precision=highest)
    range_t = lax.psum(partial_range, "col")
    gram = jnp.einsum("arp,asp->ars", range_t, range_t, precision=highest) / width
    basis = tri_solve(jnp.linalg.cholesky(gram), range_t)
    projected_part = jnp.einsum("arp,apq->arq", basis, updated, precision=highest)
    projected = lax.all_gather(projected_part, "col", axis=2, tiled=True)
    permuted = jnp.take(projected, perm, axis=2)
    coeff = pair_apply(permuted, pair_kind, pivot_values) / jnp.sqrt(jnp.float32(width))
    return (trail_out, basis[:, None], coeff[:, None])


def solution(mesh):
    return jax.shard_map(
        body,
        mesh=mesh,
        in_specs=(
            P(None, "row", None, None, "col", None),
            P(None, "row", None, "col"),
            P(None, "row", None, "col"),
            P(None, "row", None, "col"),
            P(None, "col", None, "row"),
            P(None, "col", None, "row"),
            P(None, "col"),
            P(),
            P(),
            P(),
            P(),
            P(),
        ),
        out_specs=(
            P(None, "row", None, None, "col", None),
            P(None, "row", None, None),
            P(None, "row", None, None),
        ),
        check_vma=False,
    )
```

profile of v0, /device:TPU:0, one launch (start us, length us, event | category | flops | bytes accessed | tf_op | source)
XLA Modules:
  0.0 159.1 jit_solution(12313392400558865005)
XLA Ops:
  7.3 0.8 broadcast_compare_fusion
  8.1 0.8 fusion.16
  8.9 0.9 copy.54
  9.8 0.9 copy.51
  10.8 1.0 copy.59
  11.8 16.5 %all_gather.15 = f32[2,1,64,512]{2,0,1,3:T(2,128)S(1)} all-gather(f32[2,1,64,64]{2,0,1,3:T(2,128)S(1)} %copy.51), channel_id=1, replica_groups=mesh['row'=4,'col'=8] {'col'}, dimensions={3}, use_global_device_ids=true | all-gather | bytes 294912 | tf_op jit(solution)/shard_map/all_gather | solution.py:50
  28.5 14.8 %all_gather.17 = f32[2,1,64,512]{2,0,1,3:T(2,128)S(1)} all-gather(f32[2,1,64,64]{2,0,1,3:T(2,128)S(1)} %copy.54), channel_id=1, replica_groups=mesh['row'=4,'col'=8] {'col'}, dimensions={3}, use_global_device_ids=true | all-gather | bytes 294912 | tf_op jit(solution)/shard_map/all_gather | solution.py:49
  43.5 2.2 %broadcast_select_fusion.4 = (f32[64,256,1]{0,2,1:T(1,128)S(1)}, f32[64,256,1]{0,2,1:T(1,128)S(1)}) fusion(pred[256]{0:T(512)(128)(4,1)S(1)} %broadcast_compare_fusion, f32[64,256,2]{0,2,1:T(2,128)S(1)} %bitcast.82, f32[256]{0:T(256)S(1)} %bitcast.90, f32[256]{0:T(256)S(1)} %bitcast.96, f32[256]{0:T(256)S(1)} %bitcast.93, f32[256]{0:T(256)S(1)} %bitcast.87), kind=kLoop, calls=%fused_computation.21 | loop fusion | flops 196608 | bytes 266496 | tf_op jit(solution)/shard_map/jit(_where)/select_n | solution.py:16
  47.7 1.1 convolution_bitcast_fusion.1
  48.9 10.3 %all_gather.18 = f32[2,1,64,512]{3,2,0,1:T(8,128)S(1)} all-gather(f32[2,1,64,128]{3,2,0,1:T(8,128)S(1)} %bitcast.85), channel_id=1, replica_groups=mesh['row'=4,'col'=8] {'row'}, dimensions={3}, use_global_device_ids=true | all-gather | bytes 327680 | tf_op jit(solution)/shard_map/all_gather | solution.py:53
  59.2 10.2 %all_gather.16 = f32[2,1,64,512]{3,2,0,1:T(8,128)S(1)} all-gather(f32[2,1,64,128]{3,2,0,1:T(8,128)S(1)} %bitcast.86), channel_id=1, replica_groups=mesh['row'=4,'col'=8] {'row'}, dimensions={3}, use_global_device_ids=true | all-gather | bytes 327680 | tf_op jit(solution)/shard_map/all_gather | solution.py:54
  69.9 0.6 convolution_bitcast_fusion
  70.5 7.2 %bitcast_subtract_fusion = f32[2,1,512,2,1,512]{5,2,0,3,4,1:T(8,128)} fusion(f32[2,1,512,2,1,512]{5,4,3,2,1,0:T(1,128)} %param.12, f32[2,512,2,64]{1,3,0,2:T(8,128)S(1)} %convolution_bitcast_fusion, f32[2,1,64,512]{3,2,0,1:T(8,128)S(1)} %all_gather.18), kind=kOutput, calls=%fused_computation.1 | convolution fusion | flops 806354944 | bytes 9175040 | tf_op jit(solution)/shard_map/apbs,bsq->apbq/dot_general | solution.py:62
  77.9 8.5 %copy.66 = f32[2,1,512,2,1,512]{5,4,3,2,1,0:T(1,128)} copy(f32[2,1,512,2,1,512]{5,2,0,3,4,1:T(8,128)} %bitcast_subtract_fusion) | data formatting | bytes 8388608
  86.4 19.4 %all-reduce.2.cloned.1.call-done = f32[2,64,512]{2,1,0:T(8,128)} async-done(((f32[2,64,512]{2,1,0:T(8,128)}), f32[2,64,512]{2,1,0:T(8,128)}) %all-reduce.2.cloned.1.call-update) | async-done | bytes 262160 | tf_op jit(solution)/shard_map/psum | solution.py:72
  105.8 1.4 fusion.17
  107.3 11.7 %custom-call.8 = f32[2,64,64]{2,1,0:T(8,128)S(1)} custom-call(f32[2,64,64]{2,1,0:T(8,128)S(1)} %fusion.14), custom_call_target="Cholesky" | custom-call | tf_op jit(solution)/shard_map/jit(cholesky)/cholesky | solution.py:74
  119.3 9.8 %custom-call.9 = f32[2,1,64,64]{2,3,1,0:T(8,128)S(1)} custom-call(f32[2,1,64,64]{3,2,1,0:T(8,128)S(1)} %select_bitcast_fusion), custom_call_target="InvertDiagBlocksLowerTriangular" | custom-call | tf_op jit(solution)/shard_map/vmap(jit(_solve_triangular))/triangular_solve | solution.py:26
  129.1 1.4 fusion.12
  131.0 15.1 %all_gather.19 = f32[2,64,512]{1,0,2:T(2,128)S(1)} all-gather(f32[2,64,64]{1,0,2:T(2,128)S(1)} %copy.64), channel_id=1, replica_groups=mesh['row'=4,'col'=8] {'col'}, dimensions={2}, use_global_device_ids=true | all-gather | bytes 294912 | tf_op jit(solution)/shard_map/all_gather | solution.py:76
  146.1 2.1 %gather_fusion = f32[512,2,64]{2,1,0:T(2,128)S(1)} fusion(f32[2,64,512]{1,0,2:T(2,128)S(1)} %all_gather.19, s32[1024]{0:T(1024)S(1)} %pad_clamp_fusion), kind=kCustom, calls=%fused_computation | custom fusion | bytes 526336 | tf_op jit(solution)/shard_map/jit(_take)/gather | solution.py:77
  148.6 2.2 %broadcast_select_fusion.1 = (f32[2,64,256,1]{1,3,2,0:T(1,128)S(1)}, f32[2,64,256,1]{1,3,2,0:T(1,128)S(1)}) fusion(pred[256]{0:T(512)(128)(4,1)S(1)} %broadcast_compare_fusion, f32[2,64,256,2]{1,3,2,0:T(2,128)S(1)} %broadcast_select_fusion.2, f32[256]{0:T(256)S(1)} %bitcast.92, f32[256]{0:T(256)S(1)} %multiply_subtract_fusion, f32[256]{0:T(256)S(1)} %bitcast.95, ...), kind=kLoop, calls=%fused_computation.9 | loop fusion | flops 393216 | bytes 528640 | tf_op jit(solution)/shard_map/jit(_where)/select_n | solution.py:16
  150.8 0.6 maximum_multiply_fusion
  151.4 0.9 copy.68
  (41 shorter events, 4.4 us)
Async XLA Ops:
  7.2 38.8 %copy-start = (f32[64,512]{1,0:T(8,128)S(1)}, f32[64,512]{1,0:T(8,128)}, u32[]{:S(2)}) copy-start(f32[64,512]{1,0:T(8,128)} %param.19) | copy-start | bytes 393220
  7.2 39.7 %copy-start.6 = (s32[512]{0:T(512)S(1)}, s32[512]{0:T(512)}, u32[]{:S(2)}) copy-start(s32[512]{0:T(512)} %param.21) | copy-start | bytes 6148
  7.2 40.1 %copy-start.5 = (f32[64,64]{1,0:T(8,128)S(1)}, f32[64,64]{1,0:T(8,128)}, u32[]{:S(2)}) copy-start(f32[64,64]{1,0:T(8,128)} %param.18) | copy-start | bytes 49156
  7.2 40.1 %copy-start.2 = (f32[2,1,512,64]{2,3,1,0:T(8,128)S(1)}, f32[2,1,512,64]{2,3,1,0:T(8,128)}, u32[]{:S(2)}) copy-start(f32[2,1,512,64]{2,3,1,0:T(8,128)} %param.13) | copy-start | bytes 786436
  7.2 41.7 %copy-start.3 = (f32[2,1,64,128]{3,2,1,0:T(8,128)S(1)}, f32[2,1,64,128]{3,2,1,0:T(8,128)}, u32[]{:S(2)}) copy-start(f32[2,1,64,128]{3,2,1,0:T(8,128)} %param.16) | copy-start | bytes 196612
  7.2 52.0 %copy-start.4 = (f32[2,1,64,128]{3,2,1,0:T(8,128)S(1)}, f32[2,1,64,128]{3,2,1,0:T(8,128)}, u32[]{:S(2)}) copy-start(f32[2,1,64,128]{3,2,1,0:T(8,128)} %param.17) | copy-start | bytes 196612
  7.2 98.6 %all-reduce.2.cloned.1.call-start = ((), (), s32[]{:S(2)}) async-start(), calls=%async_computation | async-start | bytes 524288 | tf_op jit(solution)/shard_map/psum | solution.py:72
  130.5 21.8 %copy-start.1 = (f32[2,64,512]{2,1,0:T(8,128)}, f32[2,64,512]{2,1,0:T(8,128)S(1)}, u32[]{:S(2)}) copy-start(f32[2,64,512]{2,1,0:T(8,128)S(1)} %fusion.12) | copy-start | bytes 786436
Sparse Core Ops, SparseCore 0:
  49.0 56.7 all-reduce.1
where the time goes:
time: 160 us; the launch traced here: 159 us
  blocking collectives  66.8 us (42%)
  other arithmetic  29.1 us (18%)
  waiting for transfers between devices  19.4 us (12%)
  local copies, waits for them, and re-layouts  15.2 us (10%)
  between operations  14.4 us (9%)
  matrix products  14.3 us (9%)
    psum x1, waiting for transfers between devices, body(): range_t = lax.psum(partial_range, 'col')  19.4 us
    all_gather x1, blocking collectives, body(): lax.all_gather(row_coeff, 'col', axis=3, tiled=True)  16.5 us
    all_gather x1, blocking collectives, body(): projected = lax.all_gather(projected_part, 'col', axis=2, tiled=True)  15.1 us
    all_gather x1, blocking collectives, body(): lax.all_gather(row_basis, 'col', axis=3, tiled=True)  14.8 us
    unnamed x19, local copies, waits for them, and re-layouts  12.3 us
    another operation x4, other arithmetic, body(): basis = tri_solve(jnp.linalg.cholesky(gram), range_t)  11.9 us
    all_gather x1, blocking collectives, body(): lax.all_gather(col_basis, 'row', axis=3, tiled=True)  10.3 us
    all_gather x1, blocking collectives, body(): lax.all_gather(col_scaled, 'row', axis=3, tiled=True)  10.2 us
  transfers between devices with their start and end apart: 1, of which 1 were waited for; matrix products, arithmetic and copies ran while one was open for 11% of the time, Pallas kernels for 0%

commit v1 on v0

--- a/solution.py
+++ b/solution.py
@@ -69,7 +69,7 @@
     selector = (perm[:, None] == column_ids[None, :]).astype(jnp.float32)
     local_sketch = jnp.dot(scaled_t, selector, precision=highest)
     partial_range = jnp.einsum("apq,rq->arp", updated, local_sketch, precision=highest)
-    range_t = lax.psum(partial_range, "col")
+    range_t = jnp.sum(lax.all_gather(partial_range, "col"), axis=0)
     gram = jnp.einsum("arp,asp->ars", range_t, range_t, precision=highest) / width
     basis = tri_solve(jnp.linalg.cholesky(gram), range_t)
     projected_part = jnp.einsum("arp,apq->arq", basis, updated, precision=highest)

time: 160 us -> 137 us (0.86)
  waiting for transfers between devices: 19.4 us -> 0.04 us
  matrix products: 14.3 us -> 11 us
  local copies, waits for them, and re-layouts: 15.2 us -> 13 us
  other arithmetic: 29.1 us -> 30.9 us
    psum x1 -> x0, waiting for transfers between devices: 19.4 us -> none  [body(): range_t = lax.psum(partial_range, 'col')]
    unnamed x19, local copies, waits for them, and re-layouts: 12.3 us -> 10.1 us
    reduce_sum x0 -> x1, other arithmetic: none -> 1.82 us  [body(): range_t = jnp.sum(lax.all_gather(partial_range, 'col'), axis=0)]
  transfers between devices with their start and end apart: 1 -> 1, of which waited for: 1 -> 0; matrix products, arithmetic and copies ran while one was open for 11% -> 10% of each run, Pallas kernels for 0% -> 0%
where the time goes in v1:
time: 137 us
  blocking collectives  67.3 us (49%)
  other arithmetic  30.9 us (23%)
  between operations  14.4 us (11%)
  local copies, waits for them, and re-layouts  13 us (9%)
  matrix products  11 us (8%)
    all_gather x1, blocking collectives, body(): lax.all_gather(row_coeff, 'col', axis=3, tiled=True)  16.5 us
    all_gather x1, blocking collectives, body(): projected = lax.all_gather(projected_part, 'col', axis=2, tiled=True)  15.5 us
    all_gather x1, blocking collectives, body(): lax.all_gather(row_basis, 'col', axis=3, tiled=True)  14.8 us
    another operation x4, other arithmetic, body(): basis = tri_solve(jnp.linalg.cholesky(gram), range_t)  11.9 us
    all_gather x1, blocking collectives, body(): lax.all_gather(col_basis, 'row', axis=3, tiled=True)  10.3 us
    all_gather x1, blocking collectives, body(): lax.all_gather(col_scaled, 'row', axis=3, tiled=True)  10.2 us
    unnamed x19, local copies, waits for them, and re-layouts  10.1 us
    another operation x3, other arithmetic, tri_solve(): jax.scipy.linalg.solve_triangular(low, right, lower=True)  9.92 us
  transfers between devices with their start and end apart: 1, of which 0 were waited for; matrix products, arithmetic and copies ran while one was open for 10% of the time, Pallas kernels for 0%

profile of v1, /device:TPU:0, one launch (start us, length us, event | category | flops | bytes accessed | tf_op | source)
XLA Modules:
  0.0 136.7 jit_solution(2824210151659662704)
XLA Ops:
  7.3 0.8 broadcast_compare_fusion
  8.1 0.8 fusion.16
  8.9 0.9 copy.54
  9.8 0.9 copy.51
  10.8 1.0 copy.59
  11.8 16.5 %all_gather.21 = f32[2,1,64,512]{2,0,1,3:T(2,128)S(1)} all-gather(f32[2,1,64,64]{2,0,1,3:T(2,128)S(1)} %copy.51), channel_id=1, replica_groups=mesh['row'=4,'col'=8] {'col'}, dimensions={3}, use_global_device_ids=true | all-gather | bytes 294912 | tf_op jit(solution)/shard_map/all_gather | solution.py:50
  28.5 14.8 %all_gather.23 = f32[2,1,64,512]{2,0,1,3:T(2,128)S(1)} all-gather(f32[2,1,64,64]{2,0,1,3:T(2,128)S(1)} %copy.54), channel_id=1, replica_groups=mesh['row'=4,'col'=8] {'col'}, dimensions={3}, use_global_device_ids=true | all-gather | bytes 294912 | tf_op jit(solution)/shard_map/all_gather | solution.py:49
  43.5 2.2 %broadcast_select_fusion.4 = (f32[64,256,1]{0,2,1:T(1,128)S(1)}, f32[64,256,1]{0,2,1:T(1,128)S(1)}) fusion(pred[256]{0:T(512)(128)(4,1)S(1)} %broadcast_compare_fusion, f32[64,256,2]{0,2,1:T(2,128)S(1)} %bitcast.84, f32[256]{0:T(256)S(1)} %bitcast.92, f32[256]{0:T(256)S(1)} %bitcast.98, f32[256]{0:T(256)S(1)} %bitcast.95, f32[256]{0:T(256)S(1)} %bitcast.89), kind=kLoop, calls=%fused_computation.21 | loop fusion | flops 196608 | bytes 266496 | tf_op jit(solution)/shard_map/jit(_where)/select_n | solution.py:16
  46.0 0.5 fusion.6
  47.8 1.1 convolution_bitcast_fusion.1
  49.0 10.3 %all_gather.24 = f32[2,1,64,512]{3,2,0,1:T(8,128)S(1)} all-gather(f32[2,1,64,128]{3,2,0,1:T(8,128)S(1)} %bitcast.87), channel_id=1, replica_groups=mesh['row'=4,'col'=8] {'row'}, dimensions={3}, use_global_device_ids=true | all-gather | bytes 327680 | tf_op jit(solution)/shard_map/all_gather | solution.py:53
  59.4 10.2 %all_gather.22 = f32[2,1,64,512]{3,2,0,1:T(8,128)S(1)} all-gather(f32[2,1,64,128]{3,2,0,1:T(8,128)S(1)} %bitcast.88), channel_id=1, replica_groups=mesh['row'=4,'col'=8] {'row'}, dimensions={3}, use_global_device_ids=true | all-gather | bytes 327680 | tf_op jit(solution)/shard_map/all_gather | solution.py:54
  69.5 0.5 fusion.1
  70.1 0.6 convolution_bitcast_fusion
  70.6 6.0 %bitcast_subtract_fusion = f32[2,1,512,2,1,512]{5,2,0,3,4,1:T(8,128)S(1)} fusion(f32[2,1,512,2,1,512]{5,4,3,2,1,0:T(1,128)} %param.12, f32[2,512,2,64]{1,3,0,2:T(8,128)S(1)} %convolution_bitcast_fusion, f32[2,1,64,512]{3,2,0,1:T(8,128)S(1)} %all_gather.24), kind=kOutput, calls=%fused_computation.1 | convolution fusion | flops 806354944 | bytes 9175040 | tf_op jit(solution)/shard_map/apbs,bsq->apbq/dot_general | solution.py:62
  76.6 6.3 %copy.66 = f32[2,1,512,2,1,512]{5,4,3,2,1,0:T(1,128)} copy(f32[2,1,512,2,1,512]{5,2,0,3,4,1:T(8,128)S(1)} %bitcast_subtract_fusion) | data formatting | bytes 8388608
  83.0 1.8 %reduce_sum.9 = f32[2,64,512]{2,1,0:T(8,128)S(1)} reduce(f32[8,2,64,512]{3,2,1,0:T(8,128)} %bitcast.80, f32[]{:T(128)} %constant.67.clone.1), dimensions={0}, to_apply=%region_0.1 | reduce | flops 458752 | bytes 2359300 | tf_op jit(solution)/shard_map/reduce_sum | solution.py:72
  85.3 11.7 %custom-call.8 = f32[2,64,64]{2,1,0:T(8,128)S(1)} custom-call(f32[2,64,64]{2,1,0:T(8,128)S(1)} %fusion.14), custom_call_target="Cholesky" | custom-call | tf_op jit(solution)/shard_map/jit(cholesky)/cholesky | solution.py:74
  97.3 9.8 %custom-call.9 = f32[2,1,64,64]{2,3,1,0:T(8,128)S(1)} custom-call(f32[2,1,64,64]{3,2,1,0:T(8,128)S(1)} %select_bitcast_fusion), custom_call_target="InvertDiagBlocksLowerTriangular" | custom-call | tf_op jit(solution)/shard_map/vmap(jit(_solve_triangular))/triangular_solve | solution.py:26
  108.0 15.5 %all_gather.27 = f32[2,64,512]{1,0,2:T(2,128)S(1)} all-gather(f32[2,64,64]{1,0,2:T(2,128)S(1)} %copy.64), channel_id=1, replica_groups=mesh['row'=4,'col'=8] {'col'}, dimensions={2}, use_global_device_ids=true | all-gather | bytes 294912 | tf_op jit(solution)/shard_map/all_gather | solution.py:76
  123.6 2.1 %gather_fusion = f32[512,2,64]{2,1,0:T(2,128)S(1)} fusion(f32[2,64,512]{1,0,2:T(2,128)S(1)} %all_gather.27, s32[1024]{0:T(1024)S(1)} %pad_clamp_fusion), kind=kCustom, calls=%fused_computation | custom fusion | bytes 526336 | tf_op jit(solution)/shard_map/jit(_take)/gather | solution.py:77
  126.1 2.2 %broadcast_select_fusion.1 = (f32[2,64,256,1]{1,3,2,0:T(1,128)S(1)}, f32[2,64,256,1]{1,3,2,0:T(1,128)S(1)}) fusion(pred[256]{0:T(512)(128)(4,1)S(1)} %broadcast_compare_fusion, f32[2,64,256,2]{1,3,2,0:T(2,128)S(1)} %broadcast_select_fusion.2, f32[256]{0:T(256)S(1)} %bitcast.94, f32[256]{0:T(256)S(1)} %multiply_subtract_fusion, f32[256]{0:T(256)S(1)} %bitcast.97, ...), kind=kLoop, calls=%fused_computation.9 | loop fusion | flops 393216 | bytes 528640 | tf_op jit(solution)/shard_map/jit(_where)/select_n | solution.py:16
  128.3 0.6 maximum_multiply_fusion
  128.9 0.9 copy.68
  (42 shorter events, 4.2 us)
Async XLA Ops:
  7.2 38.8 %copy-start = (f32[64,512]{1,0:T(8,128)S(1)}, f32[64,512]{1,0:T(8,128)}, u32[]{:S(2)}) copy-start(f32[64,512]{1,0:T(8,128)} %param.19) | copy-start | bytes 393220
  7.2 39.7 %copy-start.6 = (s32[512]{0:T(512)S(1)}, s32[512]{0:T(512)}, u32[]{:S(2)}) copy-start(s32[512]{0:T(512)} %param.21) | copy-start | bytes 6148
  7.2 40.1 %copy-start.5 = (f32[64,64]{1,0:T(8,128)S(1)}, f32[64,64]{1,0:T(8,128)}, u32[]{:S(2)}) copy-start(f32[64,64]{1,0:T(8,128)} %param.18) | copy-start | bytes 49156
  7.2 40.1 %copy-start.2 = (f32[2,1,512,64]{2,3,1,0:T(8,128)S(1)}, f32[2,1,512,64]{2,3,1,0:T(8,128)}, u32[]{:S(2)}) copy-start(f32[2,1,512,64]{2,3,1,0:T(8,128)} %param.13) | copy-start | bytes 786436
  7.2 41.8 %copy-start.3 = (f32[2,1,64,128]{3,2,1,0:T(8,128)S(1)}, f32[2,1,64,128]{3,2,1,0:T(8,128)}, u32[]{:S(2)}) copy-start(f32[2,1,64,128]{3,2,1,0:T(8,128)} %param.16) | copy-start | bytes 196612
  7.2 52.2 %copy-start.4 = (f32[2,1,64,128]{3,2,1,0:T(8,128)S(1)}, f32[2,1,64,128]{3,2,1,0:T(8,128)}, u32[]{:S(2)}) copy-start(f32[2,1,64,128]{3,2,1,0:T(8,128)} %param.17) | copy-start | bytes 196612
  7.2 75.8 %all-gather.3.cloned.1.call-start = ((), (), s32[]{:S(2)}) async-start(), calls=%async_computation | async-start | bytes 2359296 | tf_op jit(solution)/shard_map/all_gather | solution.py:72
  107.6 22.3 %copy-start.1 = (f32[2,64,512]{2,1,0:T(8,128)}, f32[2,64,512]{2,1,0:T(8,128)S(1)}, u32[]{:S(2)}) copy-start(f32[2,64,512]{2,1,0:T(8,128)S(1)} %fusion.12) | copy-start | bytes 786436
Sparse Core Ops, SparseCore 0:
  49.0 30.5 all-gather.2
